TPU v7x, 256 devices: a whole 4x4x8 slice. The times are simulated.
256 devices in a mesh: rows: 8 (over y, x_lo), cols: 32 (over x_hi, z, core).
Axes of the slice: x: 4 (x_hi: 2, x_lo: 2; x = x_hi * 2 + x_lo), y: 4, z: 8, core: 2. Of those that a mesh axis runs over, the one named last changes fastest.
Arguments:
- interaction: bfloat16 [16384, 8192], P('rows', 'cols'), may hold values from -0.125 to 0.125
- commands: bfloat16 [1024, 8192], P('rows', 'cols'), may hold values from -6 to 6
- slopes_measured: bfloat16 [16384, 1024], P(('rows', 'cols')), may hold values from -6 to 6
- frame_lag: int32 [1], replicated, may hold values from 1 to 256
- frame_count: int32 [1], replicated, may hold values from 256 to 1024
Outputs:
- lag_covariance: float32 [16384, 16384], P('rows', 'cols')
All inputs are finite; a program needn't handle non-finite values.
Results may differ from a plain program's by a relative error of at most 0.004.
Values may be sent and summed in bfloat16 or wider, within the bound.
A program may use at most 64 MiB of HBM per device.

v0:
```python
import math

import jax
import jax.numpy as jnp
from jax import lax
from jax.sharding import PartitionSpec as P

FRAMES = 1024


def rows_for(lines, devices):
    spare = -len(lines) % devices
    return jnp.pad(lines, [(0, spare)] + [(0, 0)] * (lines.ndim - 1))


def spread(value, axis, root):
    lines = jnp.where(lax.axis_index(axis) == root, value, jnp.zeros_like(value)).reshape(
        -1, *value.shape[1:][-1:]
    )
    padded = rows_for(lines, lax.axis_size(axis))
    own = lax.psum_scatter(padded, axis, scatter_dimension=0, tiled=True)
    return lax.all_gather(own, axis, axis=0, tiled=True)[: len(lines)].reshape(value.shape)


def delay_frames(response, frame_lag):
    margin = FRAMES // 4
    padded = jnp.concatenate(
        [jnp.zeros((response.shape[0], margin), response.dtype), response], axis=1
    )
    return lax.dynamic_slice_in_dim(padded, margin - frame_lag[0], FRAMES, 1)


def mask_frames(summed, frame_count):
    frame_index = lax.broadcasted_iota(jnp.int32, summed.shape, 1)
    return jnp.where(frame_index < frame_count[0], summed, 0.0).astype(jnp.bfloat16)


def local(interaction, commands, slopes_measured, frame_lag, frame_count):
    gathered = lax.all_gather(commands, "rows", axis=0, tiled=True)
    local_rows = slopes_measured.shape[0]
    column_index = lax.axis_index("cols")
    response = delay_frames(
        lax.dot_general(
            interaction, gathered, (((1,), (1,)), ((), ())), preferred_element_type=jnp.float32
        ),
        frame_lag,
    )
    offset = column_index * local_rows
    measured = lax.dynamic_update_slice_in_dim(
        jnp.zeros_like(response), slopes_measured.astype(jnp.float32), offset, 0
    )
    summed = lax.psum(response + measured, "cols")
    openloop = mask_frames(summed, frame_count)
    blocks_per = lax.axis_size("cols") // lax.axis_size("rows")
    piece_width = openloop.shape[0] // blocks_per
    column_piece = lax.dynamic_slice_in_dim(
        openloop, column_index % blocks_per * piece_width, piece_width, 0
    )
    column_slopes = spread(column_piece, "rows", column_index // blocks_per)
    advanced = jnp.concatenate(
        [openloop[:, 1:], jnp.zeros((openloop.shape[0], 1), jnp.bfloat16)], axis=1
    )
    scaling = 1.0 / math.sqrt(FRAMES)
    lagged_tile = lax.dot_general(
        advanced, column_slopes, (((1,), (1,)), ((), ())), preferred_element_type=jnp.float32
    )
    return lagged_tile * scaling


def solution(mesh):
    return jax.shard_map(
        local,
        mesh=mesh,
        in_specs=(P("rows", "cols"), P("rows", "cols"), P(("rows", "cols"), None), P(), P()),
        out_specs=P("rows", "cols"),
        check_vma=False,
    )
```

profile of v0, /device:TPU:1, one launch (start us, length us, event | category | flops | bytes accessed | tf_op | source)
XLA Modules:
  0.0 309.2 jit_solution(13493733871164470045)
XLA Ops:
  6.5 0.0 copy-start
  6.5 0.0 reduce-scatter.2.cloned.1.call-start
  7.3 25.7 %all_gather.6 = bf16[1024,256]{1,0:T(8,128)(2,1)S(1)} all-gather(bf16[128,256]{1,0:T(8,128)(2,1)} %param.6), channel_id=1, replica_groups=mesh['rows'=8,'cols'=32] {'rows'}, dimensions={0}, use_global_device_ids=true | all-gather | bytes 589824 | tf_op jit(solution)/shard_map/all_gather | solution.py:39
  33.0 0.0 copy-done
  33.0 1.3 fusion.8
  34.3 0.0 copy-start.1
  34.3 3.2 %copy-done.1 = f32[2048,1024]{1,0:T(8,128)} copy-done((f32[2048,1024]{1,0:T(8,128)}, f32[2048,1024]{1,0:T(8,128)S(1)}, u32[]{:S(2)}) %copy-start.1) | copy-done | bytes 8388632
  37.5 0.0 copy-start.3
  37.5 5.4 %pad_dynamic-slice_fusion.1 = f32[2048,1024]{1,0:T(8,128)} fusion(s32[]{:T(128)S(6)} %select_n.36, f32[2048,1024]{1,0:T(8,128)S(1)} %fusion.8), kind=kLoop, calls=%fused_computation.1 | loop fusion | bytes 16777220 | tf_op jit(solution)/shard_map/dynamic_slice | solution.py:30
  43.0 0.0 copy-done.3
  43.0 1.8 fusion.6
  44.8 162.0 %all-reduce.3 = bf16[2048,1024]{1,0:T(8,128)(2,1)} all-reduce(f32[2048,1024]{1,0:T(8,128)} %fusion.6), channel_id=1, replica_groups=mesh['rows'=8,'cols'=32] {'cols'}, use_global_device_ids=true, to_apply=%region_0.0 | all-reduce | flops 2097152 | bytes 12582912 | tf_op jit(solution)/shard_map/psum | solution.py:52
  207.5 3.4 %select_convert_fusion = bf16[2048,1024]{1,0:T(8,128)(2,1)S(1)} fusion(bf16[2048,1024]{1,0:T(8,128)(2,1)} %all-reduce.3, pred[1024]{0:T(1024)(128)(4,1)S(1)} %iota_compare_fusion), kind=kLoop, calls=%fused_computation.2 | loop fusion | flops 2097152 | bytes 8389632 | tf_op jit(solution)/shard_map/convert_element_type | solution.py:35
  210.9 0.0 copy-start.2
  210.9 2.0 copy-done.2
  212.9 1.2 dynamic-slice_select_fusion
  214.0 0.0 reduce-scatter.2.cloned.1.call-update
  214.1 0.0 all-gather.2.cloned.1.call-start
  214.1 38.0 %reduce-scatter.2.cloned.1.call-done = bf16[64,1024]{1,0:T(8,128)(2,1)} async-done(((bf16[512,1024]{1,0:T(8,128)(2,1)}), bf16[64,1024]{1,0:T(8,128)(2,1)}) %reduce-scatter.2.cloned.1.call-update) | async-done | bytes 131088 | tf_op jit(solution)/shard_map/reduce_scatter | solution.py:21
  252.1 0.0 all-gather.2.cloned.1.call-update
  252.2 6.5 %slice.4 = bf16[2048,1023]{1,0:T(8,128)(2,1)} slice(bf16[2048,1024]{1,0:T(8,128)(2,1)} %copy-done.2), slice={[0:2048], [1:1024]} | slice | bytes 8380416 | tf_op jit(solution)/shard_map/slice | solution.py:61
  258.7 36.8 %all-gather.2.cloned.1.call-done = bf16[512,1024]{1,0:T(8,128)(2,1)} async-done(((bf16[64,1024]{1,0:T(8,128)(2,1)}), bf16[512,1024]{1,0:T(8,128)(2,1)}) %all-gather.2.cloned.1.call-update) | async-done | bytes 1048592 | tf_op jit(solution)/shard_map/all_gather | solution.py:22
  295.5 6.9 %fusion.2 = f32[2048,512]{1,0:T(8,128)} fusion(bf16[512,1024]{1,0:T(8,128)(2,1)} %all-gather.2.cloned.1.call-done, bf16[2048,1023]{1,0:T(8,128)(2,1)} %slice.4), kind=kOutput, calls=%fused_computation.5 | convolution fusion | flops 2148532224 | bytes 9433088 | tf_op jit(solution)/shard_map/dot_general | solution.py:64
  (1 shorter events, 0.0 us)
Async XLA Ops:
  6.5 26.5 %copy-start = (bf16[2048,256]{1,0:T(8,128)(2,1)S(1)}, bf16[2048,256]{1,0:T(8,128)(2,1)}, u32[]{:S(2)}) copy-start(bf16[2048,256]{1,0:T(8,128)(2,1)} %param.5) | copy-start | bytes 3145732
  6.5 245.6 %reduce-scatter.2.cloned.1.call-start = ((), (), s32[]{:S(2)}) async-start(), calls=%async_computation.1 | async-start | bytes 1179648 | tf_op jit(solution)/shard_map/reduce_scatter | solution.py:21
  34.3 3.2 %copy-start.1 = (f32[2048,1024]{1,0:T(8,128)}, f32[2048,1024]{1,0:T(8,128)S(1)}, u32[]{:S(2)}) copy-start(f32[2048,1024]{1,0:T(8,128)S(1)} %fusion.8) | copy-start | bytes 25165828
  37.5 5.4 %copy-start.3 = (bf16[64,1024]{1,0:T(8,128)(2,1)S(1)}, bf16[64,1024]{1,0:T(8,128)(2,1)}, u32[]{:S(2)}) copy-start(bf16[64,1024]{1,0:T(8,128)(2,1)} %param.7) | copy-start | bytes 393220
  210.9 2.0 copy-start.2
  214.1 81.4 %all-gather.2.cloned.1.call-start = ((), (), s32[]{:S(2)}) async-start(), calls=%async_computation.2 | async-start | bytes 1179648 | tf_op jit(solution)/shard_map/all_gather | solution.py:22
Sparse Core Ops, SparseCore 0:
  214.2 37.9 reduce-scatter.1
  253.9 41.5 all-gather.1
where the time goes:
time: 314 us; the launch traced here: 309 us
  blocking collectives  188 us (60%)
  waiting for transfers between devices  74.9 us (24%)
  local copies, waits for them, and re-layouts  17.2 us (5%)
  between operations  14.9 us (5%)
  matrix products  8.17 us (3%)
  other arithmetic  6.34 us (2%)
    psum x1, blocking collectives, local(): summed = lax.psum(response + measured, 'cols')  162 us
    reduce_scatter x1, waiting for transfers between devices, spread(): own = lax.psum_scatter(padded, axis, scatter_dimension=0, tiled=True)  38 us
    all_gather x1, waiting for transfers between devices, spread(): lax.all_gather(own, axis, axis=0, tiled=True)[:len(lines)]  36.8 us
    all_gather x1, blocking collectives, local(): gathered = lax.all_gather(commands, 'rows', axis=0, tiled=True)  25.7 us
    dot_general x1, matrix products, local(): lax.dot_general(advanced, column_slopes, (((1,), (1,)), ((), ())), prefer...  6.88 us
    slice x1, local copies, waits for them, and re-layouts, local(): openloop[:, 1:]  6.51 us
  transfers between devices with their start and end apart: 2, of which 2 were waited for; matrix products, arithmetic and copies ran while one was open for 2% of the time, Pallas kernels for 0%

commit v1 on v0

v1 whole, which is shorter than its diff:
```python
import math

import jax
import jax.numpy as jnp
from jax import lax
from jax.experimental import pallas as pl
from jax.experimental.pallas import tpu as pltpu
from jax.sharding import PartitionSpec as P

FRAMES = 1024
CHUNK = 256
CHUNKS = FRAMES // CHUNK
BF, F32 = jnp.bfloat16, jnp.float32
VMEM = pl.BlockSpec(memory_space=pltpu.VMEM)
Y_ORDER = (0, 1, 3, 2)
HOPS = {"L": (BF, BF, F32, F32), "S": (BF, BF, F32)}


class Place:
    def __init__(self):
        self.r = lax.axis_index("rows")
        self.c = lax.axis_index("cols")
        self.y, self.xl = self.r // 2, self.r % 2
        self.xh, self.z, self.core = self.c // 16, (self.c // 2) % 8, self.c % 2
        self.sign = 1 - 2 * self.core

    def col(self, xh, z, core):
        return xh * 16 + z * 2 + core

    def at_z(self, dz):
        return self.r, self.col(self.xh, (self.z + dz + 16) % 8, self.core)

    def at_y(self, dy):
        return (self.r + 2 * dy + 8) % 8, self.c

    def x_far(self):
        return self.r, (self.c + 16) % 32

    def x_near(self):
        return self.y * 2 + (1 - self.xl), self.c

    def other_core(self):
        return self.r, self.c + self.sign


class Net:
    def __init__(self, send_sem, recv_sem):
        self.send_sem, self.recv_sem = send_sem, recv_sem
        self.copies = {}

    def send(self, key, src, dst, device):
        n = len(self.copies)
        copy = pltpu.make_async_remote_copy(
            src_ref=src,
            dst_ref=dst,
            send_sem=self.send_sem.at[n],
            recv_sem=self.recv_sem.at[n],
            device_id=device,
            device_id_type=pl.DeviceIdType.MESH,
        )
        copy.start()
        self.copies[key] = [copy, False]

    def wait(self, key):
        entry = self.copies[key]
        assert not entry[1]
        entry[0].wait_recv()
        entry[1] = True

    def finish(self):
        for copy, received in self.copies.values():
            assert received
            copy.wait_send()


def greet(devices):
    barrier = pltpu.get_barrier_semaphore()
    for device in devices:
        pl.semaphore_signal(barrier, inc=1, device_id=device, device_id_type=pl.DeviceIdType.MESH)
    pl.semaphore_wait(barrier, len(devices))


def reduce_kernel(a_ref, d_ref, r_ref, a2, dg, p, sb, rb, sf, rf, fin, xr, send_sem, recv_sem):
    me = Place()
    r, z, sign = me.r, me.z, me.sign
    greet(
        [me.other_core(), me.x_near(), me.x_far(), me.at_z(1), me.at_z(-1)]
        + [me.at_y(d) for d in (1, 2, 3)]
    )
    net = Net(send_sem, recv_sem)
    near = me.y * 2 + (1 - me.xl)
    net.send("d_near", d_ref, dg.at[0, r], me.x_near())
    net.send("d_core", d_ref, dg.at[1, r], me.other_core())
    net.send("a", a_ref.at[:, :, 1 - me.core], a2, me.other_core())
    for o in Y_ORDER[1:]:
        net.send(("d_y", o), d_ref, dg.at[0, r], me.at_y(-o))
    dg[0, r] = d_ref[...]
    net.wait("d_near")
    net.send("d_near_core", dg.at[0, near], dg.at[1, near], me.other_core())
    for o in Y_ORDER[1:]:
        net.send(("d_near_y", o), dg.at[0, near], dg.at[0, near], me.at_y(-o))

    def y_of(f):
        return (me.y + Y_ORDER[f]) % 4

    def product(f):
        o = Y_ORDER[f]
        if f == 0:
            net.wait("d_core")
            net.wait("a")
            net.wait("d_near_core")
        else:
            net.wait(("d_y", o))
            net.wait(("d_near_y", o))
            two = pl.ds(y_of(f) * 2, 2)
            net.send(("d_y_core", o), dg.at[0, two], dg.at[1, two], me.other_core())
            net.wait(("d_y_core", o))
        mine = dg[0, pl.ds(y_of(f) * 2, 2)].reshape(CHUNK, 256)
        others = dg[1, pl.ds(y_of(f) * 2, 2)].reshape(CHUNK, 256)
        contract = (((1,), (1,)), ((), ()))
        for xh in range(2):
            own = lax.dot_general(
                a_ref[xh, :, me.core].reshape(512, 256), mine, contract, preferred_element_type=F32
            )
            rest = lax.dot_general(
                a2[xh].reshape(512, 256), others, contract, preferred_element_type=F32
            )
            p[f, xh] = (own + rest).reshape(8, 64, CHUNK)

    slots = {}
    for way, kinds in HOPS.items():
        for hop, kind in enumerate(kinds, 1):
            slots[way, hop] = (kind, sum(1 for k, _ in slots.values() if k is kind))

    def buffer(f, way, hop, sending):
        kind, n = slots[way, hop]
        if kind is BF:
            return (sb if sending else rb).at[f, n]
        return (sf if sending else rf).at[f, n]

    def hop_on(f, way, hop):
        hops = len(HOPS[way])
        step = sign if way == "L" else -sign
        owner = (z + step * (hops + 1 - hop) + 16) % 8
        value = p[f, :, owner]
        if hop > 1:
            net.wait((f, way, hop - 1))
            value += buffer(f, way, hop - 1, False)[...].astype(F32)
        out = buffer(f, way, hop, True)
        out[...] = value.astype(HOPS[way][hop - 1])
        net.send((f, way, hop), out, buffer(f, way, hop, False), me.at_z(step))

    def total(f):
        value = p[f, :, z]
        for way in HOPS:
            net.wait((f, way, len(HOPS[way])))
            value += buffer(f, way, len(HOPS[way]), False)[...]
        fin[f] = value
        net.send((f, "x"), fin.at[f, 1 - me.xh], xr.at[f], me.x_far())

    def store(f):
        net.wait((f, "x"))
        r_ref[:, pl.ds(pl.multiple_of(y_of(f) * CHUNK, CHUNK), CHUNK)] = fin[f, me.xh] + xr[f]

    for turn in range(CHUNKS + 5):
        for f in range(CHUNKS):
            stage = turn - f
            if stage == 0:
                product(f)
                hop_on(f, "L", 1)
                hop_on(f, "S", 1)
            elif stage in (1, 2, 3):
                hop_on(f, "L", stage + 1)
                if stage < 3:
                    hop_on(f, "S", stage + 1)
            elif stage == 4:
                total(f)
            elif stage == 5:
                store(f)
    net.finish()


def gather_kernel(o_ref, osh_ref, rows_ref, cols_ref, send_sem, recv_sem):
    me = Place()
    r, c, z, xh = me.r, me.c, me.z, me.xh
    target = ((c + 4) % 8, r * 4 + c // 8)
    source = (c // 4, (c % 4) * 8 + (r + 4) % 8)
    greet(
        [me.other_core(), me.x_near(), me.x_far(), me.at_z(1), me.at_z(-1), me.at_y(1), me.at_y(-1)]
        + [target, source]
    )
    net = Net(send_sem, recv_sem)
    first, second = pl.ds(0, 32), pl.ds(32, 32)
    hops = {"L": 4, "S": 3}
    step = {"L": me.sign, "S": -me.sign}

    def slot(other, dz):
        return me.col((1 - xh) if other else xh, (z + dz + 16) % 8, me.core)

    def pass_on(key, n, half, device):
        piece = rows_ref.at[n, half]
        net.send(key, piece, piece, device)

    net.send("x1", o_ref.at[first], rows_ref.at[c, first], me.x_far())
    net.send("permute", osh_ref, cols_ref.at[c % 8], target)
    for way in hops:
        net.send(("z2", way, 1), o_ref.at[second], rows_ref.at[c, second], me.at_z(step[way]))
    for way in hops:
        net.send(("z1", way, 1), o_ref.at[first], rows_ref.at[c, first], me.at_z(step[way]))
    net.send(("x2", "own", 0), o_ref.at[second], rows_ref.at[c, second], me.x_far())
    net.send("core_own", o_ref, rows_ref.at[c], me.other_core())
    rows_ref[c] = o_ref[...]
    net.wait("x1")
    for way in hops:
        pass_on(("z1p", way, 1), slot(True, 0), first, me.at_z(step[way]))

    def to_core(key, n):
        net.send(key, rows_ref.at[n], rows_ref.at[n], me.other_core())

    def col_slot(row):
        return (row + 4) % 8

    def pass_col(key, row, device):
        piece = cols_ref.at[col_slot(row)]
        net.send(key, piece, piece, device)

    near = me.y * 2 + (1 - me.xl)
    for t in range(1, 5):
        for way in hops:
            if t > hops[way]:
                continue
            n, m = slot(False, -step[way] * t), slot(True, -step[way] * t)
            ahead = me.at_z(step[way])
            net.wait(("z2", way, t))
            if t < hops[way]:
                pass_on(("z2", way, t + 1), n, second, ahead)
            pass_on(("x2", way, t), n, second, me.x_far())
            net.wait(("z1", way, t))
            if t < hops[way]:
                pass_on(("z1", way, t + 1), n, first, ahead)
            to_core(("core", way, t), n)
            net.wait(("z1p", way, t))
            if t < hops[way]:
                pass_on(("z1p", way, t + 1), m, first, ahead)
        if t == 1:
            net.wait("permute")
            pass_col("near", r, me.x_near())
            pass_col(("y0", 1), r, me.at_y(1))
            pass_col(("y0", -1), r, me.at_y(-1))
        if t == 2:
            net.wait("near")
            pass_col(("y1", 1), near, me.at_y(1))
            pass_col(("y1", -1), near, me.at_y(-1))
        if t == 3:
            net.wait(("y0", 1))
            pass_col(("y2", 1), (r + 6) % 8, me.at_y(1))
            net.wait(("y1", -1))
            pass_col(("y2", -1), (near + 2) % 8, me.at_y(-1))
    net.wait(("x2", "own", 0))
    to_core(("core_far", "own", 0), slot(True, 0))
    for t in range(1, 5):
        for way in hops:
            if t <= hops[way]:
                net.wait(("x2", way, t))
                to_core(("core_far", way, t), slot(True, -step[way] * t))
    for key in [("y0", -1), ("y1", 1), ("y2", 1), ("y2", -1), "core_own"]:
        net.wait(key)
    for key, entry in net.copies.items():
        if not entry[1]:
            net.wait(key)
    net.finish()


def reduced(interaction, commands):
    kinds = [kind for way in HOPS.values() for kind in way]
    n_bf, n_f32 = kinds.count(BF), kinds.count(F32)
    piece = (2, 64, CHUNK)
    copies = 6 + 3 * (len(Y_ORDER) - 1) + CHUNKS * (len(kinds) + 1)
    return pl.pallas_call(
        reduce_kernel,
        out_shape=jax.ShapeDtypeStruct((64, FRAMES), F32),
        in_specs=[VMEM] * 2,
        out_specs=VMEM,
        scratch_shapes=[
            pltpu.VMEM((2, 8, 64, 256), BF),
            pltpu.VMEM((2, 8, 128, 256), BF),
            pltpu.VMEM((CHUNKS, 2, 8, 64, CHUNK), F32),
            pltpu.VMEM((CHUNKS, n_bf) + piece, BF),
            pltpu.VMEM((CHUNKS, n_bf) + piece, BF),
            pltpu.VMEM((CHUNKS, n_f32) + piece, F32),
            pltpu.VMEM((CHUNKS, n_f32) + piece, F32),
            pltpu.VMEM((CHUNKS,) + piece, F32),
            pltpu.VMEM((CHUNKS, 64, CHUNK), F32),
            pltpu.SemaphoreType.DMA((copies,)),
            pltpu.SemaphoreType.DMA((copies,)),
        ],
        compiler_params=pltpu.CompilerParams(collective_id=0, has_side_effects=True),
        name="reduce_slopes",
    )(interaction.reshape(2, 8, 2, 64, 256), commands)


def gathered(openloop, shifted):
    return pl.pallas_call(
        gather_kernel,
        out_shape=(
            jax.ShapeDtypeStruct((32, 64, FRAMES), BF),
            jax.ShapeDtypeStruct((8, 64, FRAMES), BF),
        ),
        in_specs=[VMEM] * 2,
        out_specs=(VMEM, VMEM),
        scratch_shapes=[pltpu.SemaphoreType.DMA((80,)), pltpu.SemaphoreType.DMA((80,))],
        compiler_params=pltpu.CompilerParams(collective_id=1, has_side_effects=True),
        name="gather_slopes",
    )(openloop, shifted)


def delay_frames(response, frame_lag):
    margin = FRAMES // 4
    padded = jnp.concatenate(
        [jnp.zeros((response.shape[0], margin), response.dtype), response], axis=1
    )
    return lax.dynamic_slice_in_dim(padded, margin - frame_lag[0], FRAMES, 1)


def mask_frames(summed, frame_count):
    frame_index = lax.broadcasted_iota(jnp.int32, summed.shape, 1)
    return jnp.where(frame_index < frame_count[0], summed, 0.0).astype(BF)


def local(interaction, commands, slopes_measured, frame_lag, frame_count):
    response = reduced(interaction, commands)
    summed = delay_frames(response, frame_lag) + slopes_measured.astype(F32)
    openloop = mask_frames(summed, frame_count)
    shifted = jnp.concatenate([jnp.zeros((64, 1), BF), openloop[:, :-1]], axis=1)
    rows, cols = gathered(openloop, shifted)
    tile = lax.dot_general(
        rows.reshape(2048, FRAMES),
        cols.reshape(512, FRAMES),
        (((1,), (1,)), ((), ())),
        preferred_element_type=F32,
    )
    return tile * (1.0 / math.sqrt(FRAMES))


def solution(mesh):
    return jax.shard_map(
        local,
        mesh=mesh,
        in_specs=(P("rows", "cols"), P("rows", "cols"), P(("rows", "cols"), None), P(), P()),
        out_specs=P("rows", "cols"),
        check_vma=False,
    )
```

time: 314 us -> 111 us (0.35); the launches traced: 309 us -> 110 us
  blocking collectives: 188 us -> 0 us
  Pallas kernels: 0 us -> 100 us
  waiting for transfers between devices: 74.9 us -> 0 us
  local copies, waits for them, and re-layouts: 17.2 us -> 0.76 us
  between operations: 14.9 us -> 1.34 us
  other arithmetic: 6.34 us -> 1.14 us
    psum x1 -> x0, blocking collectives: 162 us -> none  [local(): summed = lax.psum(response + measured, 'cols')]
    pallas_call x0 -> x2, Pallas kernels: none -> 100 us  [the longest x1 54.7 us: reduced(): pl.pallas_call(reduce_kernel, out_shape=jax.ShapeDtypeStruct((64, FRAMES)...]
    reduce_scatter x1 -> x0, waiting for transfers between devices: 38 us -> none  [spread(): own = lax.psum_scatter(padded, axis, scatter_dimension=0, tiled=True)]
    all_gather x1 -> x0, waiting for transfers between devices: 36.8 us -> none  [spread(): lax.all_gather(own, axis, axis=0, tiled=True)[:len(lines)]]
    all_gather x1 -> x0, blocking collectives: 25.7 us -> none  [local(): gathered = lax.all_gather(commands, 'rows', axis=0, tiled=True)]
    slice x1 -> x0, local copies, waits for them, and re-layouts: 6.51 us -> none  [local(): openloop[:, 1:]]
    dynamic_slice x1 -> x0, local copies, waits for them, and re-layouts: 5.44 us -> none  [delay_frames(): return lax.dynamic_slice_in_dim(padded, margin - frame_lag[0], FRAMES, 1)]
    unnamed x8 -> x2, local copies, waits for them, and re-layouts: 5.23 us -> 0.01 us
  transfers between devices with their start and end apart: 2 -> 0, of which waited for: 2 -> 0; matrix products, arithmetic and copies ran while one was open for 2% -> 0% of each run, Pallas kernels for 0% -> 0%
where the time goes in v1:
time: 111 us; the launch traced here: 110 us
  Pallas kernels  100 us (90%)
  matrix products  6.88 us (6%)
  between operations  1.34 us (1%)
  other arithmetic  1.14 us (1%)
    pallas_call x1, Pallas kernels, reduced(): pl.pallas_call(reduce_kernel, out_shape=jax.ShapeDtypeStruct((64, FRAMES)...  54.7 us
    pallas_call x1, Pallas kernels, gathered(): pl.pallas_call(gather_kernel, out_shape=(jax.ShapeDtypeStruct((32, 64, FR...  45.6 us
    dot_general x1, matrix products, local(): lax.dot_general(rows.reshape(2048, FRAMES), cols.reshape(512, FRAMES), ((...  6.88 us

profile of v1, /device:TPU:1, one launch (start us, length us, event | category | flops | bytes accessed | tf_op | source)
XLA Modules:
  0.0 110.4 jit_solution(4102987088616051872)
XLA Ops:
  1.3 54.7 %reduce_slopes.1 = f32[64,1024]{1,0:T(8,128)} custom-call(bf16[2,8,2,64,256]{4,3,2,1,0:T(8,128)(2,1)} %bitcast.11, bf16[128,256]{1,0:T(8,128)(2,1)} %d_ref.1), custom_call_target="tpu_custom_call" | custom-call | tf_op jit(solution)/shard_map/reduce_slopes/pallas_call | solution.py:279
  56.0 1.1 %fusion.2.o_ref = bf16[64,1024]{1,0:T(8,128)(2,1)S(1)} fusion(s32[]{:T(128)S(6)} %select_n.7, f32[64,1024]{1,0:T(8,128)} %reduce_slopes.1, bf16[64,1024]{1,0:T(8,128)(2,1)} %param.7, pred[1024]{0:T(1024)(128)(4,1)S(1)} %iota_compare_fusion), kind=kLoop, calls=%fused_computation.4 | loop fusion | flops 262144 | bytes 525316 | tf_op jit(solution)/shard_map/convert_element_type | solution.py:327
  57.2 0.0 copy-start
  57.2 0.7 concatenate.7.osh_ref
  57.9 0.0 copy-done
  57.9 45.6 %gather_slopes.1 = (bf16[32,64,1024]{2,1,0:T(8,128)(2,1)}, bf16[8,64,1024]{2,1,0:T(8,128)(2,1)}) custom-call(bf16[64,1024]{1,0:T(8,128)(2,1)} %copy-done, bf16[64,1024]{1,0:T(8,128)(2,1)} %concatenate.7.osh_ref), custom_call_target="tpu_custom_call" | custom-call | tf_op jit(solution)/shard_map/gather_slopes/pallas_call | solution.py:303
  103.5 6.9 %convolution_multiply_fusion = f32[2048,512]{1,0:T(8,128)} fusion(bf16[2048,1024]{1,0:T(8,128)(2,1)} %bitcast.12, bf16[512,1024]{1,0:T(8,128)(2,1)} %bitcast.13), kind=kOutput, calls=%fused_computation | convolution fusion | flops 2148532224 | bytes 9437184 | tf_op jit(solution)/shard_map/dot_general | solution.py:336
  (1 shorter events, 0.0 us)
Async XLA Ops:
  57.2 0.8 copy-start

commit v2 on v1

--- a/solution.py
+++ b/solution.py
@@ -14,6 +14,7 @@
 VMEM = pl.BlockSpec(memory_space=pltpu.VMEM)
 Y_ORDER = (0, 1, 3, 2)
 HOPS = {"L": (BF, BF, F32, F32), "S": (BF, BF, F32)}
+A_ORDER = (("L", 1), ("S", 1), ("L", 2), ("S", 2), ("L", 3), ("S", 3), ("L", 4), ("L", 5))
 
 
 class Place:
@@ -35,6 +36,12 @@
 
     def x_far(self):
         return self.r, (self.c + 16) % 32
+
+    def x_far_core(self):
+        return self.r, self.col(1 - self.xh, self.z, 1 - self.core)
+
+    def x_cross(self):
+        return self.y * 2 + (1 - self.xl), (self.c + 16) % 32
 
     def x_near(self):
         return self.y * 2 + (1 - self.xl), self.c
@@ -80,52 +87,88 @@
     pl.semaphore_wait(barrier, len(devices))
 
 
-def reduce_kernel(a_ref, d_ref, r_ref, a2, dg, p, sb, rb, sf, rf, fin, xr, send_sem, recv_sem):
+def reduce_kernel(a_ref, d_ref, r_ref, a4, dg, sb, rb, sf, rf, send_sem, recv_sem):
     me = Place()
-    r, z, sign = me.r, me.z, me.sign
+    r, z, xh, core, sign = me.r, me.z, me.xh, me.core, me.sign
     greet(
-        [me.other_core(), me.x_near(), me.x_far(), me.at_z(1), me.at_z(-1)]
-        + [me.at_y(d) for d in (1, 2, 3)]
+        [me.other_core(), me.x_near(), me.x_far(), me.x_cross(), me.x_far_core(), me.at_z(1), me.at_z(-1)]
+        + [me.at_y(1), me.at_y(-1)]
     )
     net = Net(send_sem, recv_sem)
     near = me.y * 2 + (1 - me.xl)
+
+    def owner(way, hop, sgn):
+        hops = len(HOPS[way])
+        return (z + (sgn if way == "L" else -sgn) * (hops + 1 - hop) + 16) % 8
+
     net.send("d_near", d_ref, dg.at[0, r], me.x_near())
+    net.send("d_cross", d_ref, dg.at[2, r], me.x_cross())
+    net.send("d_far", d_ref, dg.at[2, r], me.x_far())
     net.send("d_core", d_ref, dg.at[1, r], me.other_core())
-    net.send("a", a_ref.at[:, :, 1 - me.core], a2, me.other_core())
-    for o in Y_ORDER[1:]:
-        net.send(("d_y", o), d_ref, dg.at[0, r], me.at_y(-o))
+    for o in (1, 3):
+        net.send(("d", 0, o), d_ref, dg.at[0, r], me.at_y(-o))
+    net.send("a_core", a_ref.at[xh, :, 1 - core], a4.at[0], me.other_core())
+    for way, hop in A_ORDER:
+        n = owner(way, hop, sign)
+        net.send(("a_far", way, hop), a_ref.at[1 - xh, n, core], a4.at[1, n], me.x_far())
+        n = owner(way, hop, -sign)
+        net.send(("a_cross", way, hop), a_ref.at[1 - xh, n, 1 - core], a4.at[2, n], me.x_far_core())
     dg[0, r] = d_ref[...]
-    net.wait("d_near")
-    net.send("d_near_core", dg.at[0, near], dg.at[1, near], me.other_core())
-    for o in Y_ORDER[1:]:
-        net.send(("d_near_y", o), dg.at[0, near], dg.at[0, near], me.at_y(-o))
+    for key, k, row in (("d_near", 0, near), ("d_cross", 2, near), ("d_far", 2, r)):
+        net.wait(key)
+        piece = dg.at[k, row]
+        for o in (1, 3):
+            net.send((key, o), piece, piece, me.at_y(-o))
+        net.send((key, "core"), piece, dg.at[k + 1, row], me.other_core())
 
     def y_of(f):
         return (me.y + Y_ORDER[f]) % 4
 
-    def product(f):
+    def commands_in(f):
         o = Y_ORDER[f]
+        two = pl.ds(y_of(f) * 2, 2)
         if f == 0:
-            net.wait("d_core")
-            net.wait("a")
-            net.wait("d_near_core")
+            for key in ("d_core", ("d_near", "core"), ("d_cross", "core"), ("d_far", "core"), "a_core"):
+                net.wait(key)
+            return
+        if o == 2:
+            net.wait("relay0")
+            net.wait("relay2")
         else:
-            net.wait(("d_y", o))
-            net.wait(("d_near_y", o))
-            two = pl.ds(y_of(f) * 2, 2)
-            net.send(("d_y_core", o), dg.at[0, two], dg.at[1, two], me.other_core())
-            net.wait(("d_y_core", o))
-        mine = dg[0, pl.ds(y_of(f) * 2, 2)].reshape(CHUNK, 256)
-        others = dg[1, pl.ds(y_of(f) * 2, 2)].reshape(CHUNK, 256)
-        contract = (((1,), (1,)), ((), ()))
-        for xh in range(2):
-            own = lax.dot_general(
-                a_ref[xh, :, me.core].reshape(512, 256), mine, contract, preferred_element_type=F32
+            for key in (("d", 0, o), ("d_near", o), ("d_cross", o), ("d_far", o)):
+                net.wait(key)
+        if o == 3:
+            net.send("relay0", dg.at[0, two], dg.at[0, two], me.at_y(1))
+        if o == 1:
+            net.send("relay2", dg.at[2, two], dg.at[2, two], me.at_y(-1))
+        for k in (0, 2):
+            net.send(("core", k, o), dg.at[k, two], dg.at[k + 1, two], me.other_core())
+        for k in (0, 2):
+            net.wait(("core", k, o))
+
+    arrived = set()
+
+    def product(f, pieces):
+        for piece in pieces:
+            if piece not in arrived:
+                arrived.add(piece)
+                net.wait(("a_far",) + piece)
+                net.wait(("a_cross",) + piece)
+        owners = [owner(way, hop, sign) for way, hop in pieces]
+        total = None
+        for k in range(4):
+            if k == 0:
+                rows = [a_ref[xh, n, core] for n in owners]
+            else:
+                rows = [a4[k - 1, n] for n in owners]
+            part = lax.dot_general(
+                jnp.concatenate(rows, axis=0),
+                dg[k, pl.ds(y_of(f) * 2, 2)].reshape(CHUNK, 256),
+                (((1,), (1,)), ((), ())),
+                preferred_element_type=F32,
             )
-            rest = lax.dot_general(
-                a2[xh].reshape(512, 256), others, contract, preferred_element_type=F32
-            )
-            p[f, xh] = (own + rest).reshape(8, 64, CHUNK)
+            total = part if total is None else total + part
+        return [total[i * 64 : (i + 1) * 64] for i in range(len(pieces))]
 
     slots = {}
     for way, kinds in HOPS.items():
@@ -138,45 +181,32 @@
             return (sb if sending else rb).at[f, n]
         return (sf if sending else rf).at[f, n]
 
-    def hop_on(f, way, hop):
-        hops = len(HOPS[way])
-        step = sign if way == "L" else -sign
-        owner = (z + step * (hops + 1 - hop) + 16) % 8
-        value = p[f, :, owner]
-        if hop > 1:
-            net.wait((f, way, hop - 1))
-            value += buffer(f, way, hop - 1, False)[...].astype(F32)
-        out = buffer(f, way, hop, True)
-        out[...] = value.astype(HOPS[way][hop - 1])
-        net.send((f, way, hop), out, buffer(f, way, hop, False), me.at_z(step))
+    def stage(f, hop):
+        if hop == 1:
+            commands_in(f)
+        pieces = [(way, hop) for way in HOPS if hop <= len(HOPS[way])]
+        for (way, _), value in zip(pieces, product(f, pieces)):
+            step = sign if way == "L" else -sign
+            if hop > 1:
+                net.wait((f, way, hop - 1))
+                value += buffer(f, way, hop - 1, False)[...].astype(F32)
+            out = buffer(f, way, hop, True)
+            out[...] = value.astype(HOPS[way][hop - 1])
+            net.send((f, way, hop), out, buffer(f, way, hop, False), me.at_z(step))
 
     def total(f):
-        value = p[f, :, z]
-        for way in HOPS:
+        (value,) = product(f, [("L", 5)])
+        for way in ("S", "L"):
             net.wait((f, way, len(HOPS[way])))
-            value += buffer(f, way, len(HOPS[way]), False)[...]
-        fin[f] = value
-        net.send((f, "x"), fin.at[f, 1 - me.xh], xr.at[f], me.x_far())
-
-    def store(f):
-        net.wait((f, "x"))
-        r_ref[:, pl.ds(pl.multiple_of(y_of(f) * CHUNK, CHUNK), CHUNK)] = fin[f, me.xh] + xr[f]
-
-    for turn in range(CHUNKS + 5):
-        for f in range(CHUNKS):
-            stage = turn - f
-            if stage == 0:
-                product(f)
-                hop_on(f, "L", 1)
-                hop_on(f, "S", 1)
-            elif stage in (1, 2, 3):
-                hop_on(f, "L", stage + 1)
-                if stage < 3:
-                    hop_on(f, "S", stage + 1)
-            elif stage == 4:
-                total(f)
-            elif stage == 5:
-                store(f)
+            value += buffer(f, way, len(HOPS[way]), False)[...].astype(F32)
+        r_ref[:, pl.ds(pl.multiple_of(y_of(f) * CHUNK, CHUNK), CHUNK)] = value
+
+    todo = [(f + (hop - 0.5 if hop > 1 else 0), f, hop) for f in range(CHUNKS) for hop in range(1, 6)]
+    for _, f, hop in sorted(todo):
+        if hop < 5:
+            stage(f, hop)
+        else:
+            total(f)
     net.finish()
 
 
@@ -226,22 +256,17 @@
 
     near = me.y * 2 + (1 - me.xl)
     for t in range(1, 5):
-        for way in hops:
-            if t > hops[way]:
-                continue
-            n, m = slot(False, -step[way] * t), slot(True, -step[way] * t)
-            ahead = me.at_z(step[way])
-            net.wait(("z2", way, t))
-            if t < hops[way]:
-                pass_on(("z2", way, t + 1), n, second, ahead)
-            pass_on(("x2", way, t), n, second, me.x_far())
-            net.wait(("z1", way, t))
-            if t < hops[way]:
-                pass_on(("z1", way, t + 1), n, first, ahead)
-            to_core(("core", way, t), n)
-            net.wait(("z1p", way, t))
-            if t < hops[way]:
-                pass_on(("z1p", way, t + 1), m, first, ahead)
+        ways = [way for way in hops if t <= hops[way]]
+        for kind, half in (("z2", second), ("z1", first), ("z1p", first)):
+            for way in ways:
+                n = slot(kind == "z1p", -step[way] * t)
+                net.wait((kind, way, t))
+                if t < hops[way]:
+                    pass_on((kind, way, t + 1), n, half, me.at_z(step[way]))
+                if kind == "z2":
+                    pass_on(("x2", way, t), n, second, me.x_far())
+                if kind == "z1":
+                    to_core(("core", way, t), n)
         if t == 1:
             net.wait("permute")
             pass_col("near", r, me.x_near())
@@ -274,23 +299,20 @@
 def reduced(interaction, commands):
     kinds = [kind for way in HOPS.values() for kind in way]
     n_bf, n_f32 = kinds.count(BF), kinds.count(F32)
-    piece = (2, 64, CHUNK)
-    copies = 6 + 3 * (len(Y_ORDER) - 1) + CHUNKS * (len(kinds) + 1)
+    piece = (64, CHUNK)
+    copies = 80
     return pl.pallas_call(
         reduce_kernel,
         out_shape=jax.ShapeDtypeStruct((64, FRAMES), F32),
         in_specs=[VMEM] * 2,
         out_specs=VMEM,
         scratch_shapes=[
-            pltpu.VMEM((2, 8, 64, 256), BF),
-            pltpu.VMEM((2, 8, 128, 256), BF),
-            pltpu.VMEM((CHUNKS, 2, 8, 64, CHUNK), F32),
+            pltpu.VMEM((3, 8, 64, 256), BF),
+            pltpu.VMEM((4, 8, 128, 256), BF),
             pltpu.VMEM((CHUNKS, n_bf) + piece, BF),
             pltpu.VMEM((CHUNKS, n_bf) + piece, BF),
             pltpu.VMEM((CHUNKS, n_f32) + piece, F32),
             pltpu.VMEM((CHUNKS, n_f32) + piece, F32),
-            pltpu.VMEM((CHUNKS,) + piece, F32),
-            pltpu.VMEM((CHUNKS, 64, CHUNK), F32),
             pltpu.SemaphoreType.DMA((copies,)),
             pltpu.SemaphoreType.DMA((copies,)),
         ],

time: 111 us -> 109 us (0.982)
  Pallas kernels: 100 us -> 98.3 us
    pallas_call x1, Pallas kernels: 45.6 us -> 42.8 us  [gathered(): pl.pallas_call(gather_kernel, out_shape=(jax.ShapeDtypeStruct((32, 64, FR...]
where the time goes in v2:
time: 109 us; the launch traced here: 108 us
  Pallas kernels  98.3 us (90%)
  matrix products  6.88 us (6%)
  between operations  1.34 us (1%)
  other arithmetic  1.17 us (1%)
    pallas_call x1, Pallas kernels, reduced(): pl.pallas_call(reduce_kernel, out_shape=jax.ShapeDtypeStruct((64, FRAMES)...  55.4 us
    pallas_call x1, Pallas kernels, gathered(): pl.pallas_call(gather_kernel, out_shape=(jax.ShapeDtypeStruct((32, 64, FR...  42.8 us
    dot_general x1, matrix products, local(): lax.dot_general(rows.reshape(2048, FRAMES), cols.reshape(512, FRAMES), ((...  6.88 us

profile of v2, /device:TPU:1, one launch (start us, length us, event | category | flops | bytes accessed | tf_op | source)
XLA Modules:
  0.0 108.4 jit_solution(10471977799749772872)
XLA Ops:
  1.3 55.4 %reduce_slopes.1 = f32[64,1024]{1,0:T(8,128)} custom-call(bf16[2,8,2,64,256]{4,3,2,1,0:T(8,128)(2,1)} %bitcast.11, bf16[128,256]{1,0:T(8,128)(2,1)} %d_ref.1), custom_call_target="tpu_custom_call" | custom-call | tf_op jit(solution)/shard_map/reduce_slopes/pallas_call | solution.py:304
  56.8 1.2 %fusion.2.o_ref = bf16[64,1024]{1,0:T(8,128)(2,1)S(1)} fusion(s32[]{:T(128)S(6)} %select_n.7, f32[64,1024]{1,0:T(8,128)} %reduce_slopes.1, bf16[64,1024]{1,0:T(8,128)(2,1)} %param.7, pred[1024]{0:T(1024)(128)(4,1)S(1)} %iota_compare_fusion), kind=kLoop, calls=%fused_computation.4 | loop fusion | flops 262144 | bytes 525316 | tf_op jit(solution)/shard_map/convert_element_type | solution.py:349
  57.9 0.0 copy-start
  57.9 0.7 concatenate.7.osh_ref
  58.7 0.0 copy-done
  58.7 42.8 %gather_slopes.1 = (bf16[32,64,1024]{2,1,0:T(8,128)(2,1)}, bf16[8,64,1024]{2,1,0:T(8,128)(2,1)}) custom-call(bf16[64,1024]{1,0:T(8,128)(2,1)} %copy-done, bf16[64,1024]{1,0:T(8,128)(2,1)} %concatenate.7.osh_ref), custom_call_target="tpu_custom_call" | custom-call | tf_op jit(solution)/shard_map/gather_slopes/pallas_call | solution.py:325
  101.5 6.9 %convolution_multiply_fusion = f32[2048,512]{1,0:T(8,128)} fusion(bf16[2048,1024]{1,0:T(8,128)(2,1)} %bitcast.12, bf16[512,1024]{1,0:T(8,128)(2,1)} %bitcast.13), kind=kOutput, calls=%fused_computation | convolution fusion | flops 2148532224 | bytes 9437184 | tf_op jit(solution)/shard_map/dot_general | solution.py:358
  (1 shorter events, 0.0 us)
Async XLA Ops:
  57.9 0.8 copy-start

commit v3 on v2

--- a/solution.py
+++ b/solution.py
@@ -9,6 +9,7 @@
 
 FRAMES = 1024
 CHUNK = 256
+MARGIN = FRAMES // 4
 CHUNKS = FRAMES // CHUNK
 BF, F32 = jnp.bfloat16, jnp.float32
 VMEM = pl.BlockSpec(memory_space=pltpu.VMEM)
@@ -36,6 +37,12 @@
 
     def x_far(self):
         return self.r, (self.c + 16) % 32
+
+    def permuted(self):
+        return (self.c + 4) % 8, self.r * 4 + self.c // 8
+
+    def permuted_from(self):
+        return self.c // 4, (self.c % 4) * 8 + (self.r + 4) % 8
 
     def x_far_core(self):
         return self.r, self.col(1 - self.xh, self.z, 1 - self.core)
@@ -87,14 +94,8 @@
     pl.semaphore_wait(barrier, len(devices))
 
 
-def reduce_kernel(a_ref, d_ref, r_ref, a4, dg, sb, rb, sf, rf, send_sem, recv_sem):
-    me = Place()
+def reduce_slopes(me, net, a_ref, d_ref, response, a4, dg, sb, rb, sf, rf):
     r, z, xh, core, sign = me.r, me.z, me.xh, me.core, me.sign
-    greet(
-        [me.other_core(), me.x_near(), me.x_far(), me.x_cross(), me.x_far_core(), me.at_z(1), me.at_z(-1)]
-        + [me.at_y(1), me.at_y(-1)]
-    )
-    net = Net(send_sem, recv_sem)
     near = me.y * 2 + (1 - me.xl)
 
     def owner(way, hop, sgn):
@@ -106,7 +107,7 @@
     net.send("d_far", d_ref, dg.at[2, r], me.x_far())
     net.send("d_core", d_ref, dg.at[1, r], me.other_core())
     for o in (1, 3):
-        net.send(("d", 0, o), d_ref, dg.at[0, r], me.at_y(-o))
+        net.send(("d", o), d_ref, dg.at[0, r], me.at_y(-o))
     net.send("a_core", a_ref.at[xh, :, 1 - core], a4.at[0], me.other_core())
     for way, hop in A_ORDER:
         n = owner(way, hop, sign)
@@ -131,16 +132,14 @@
             for key in ("d_core", ("d_near", "core"), ("d_cross", "core"), ("d_far", "core"), "a_core"):
                 net.wait(key)
             return
-        if o == 2:
-            net.wait("relay0")
-            net.wait("relay2")
-        else:
-            for key in (("d", 0, o), ("d_near", o), ("d_cross", o), ("d_far", o)):
-                net.wait(key)
-        if o == 3:
-            net.send("relay0", dg.at[0, two], dg.at[0, two], me.at_y(1))
-        if o == 1:
-            net.send("relay2", dg.at[2, two], dg.at[2, two], me.at_y(-1))
+        for key, k, side in (("d", 0, me.xl), ("d_near", 0, 1 - me.xl), ("d_cross", 2, 1 - me.xl), ("d_far", 2, me.xl)):
+            if o == 2:
+                net.wait(("relay", key))
+                continue
+            net.wait((key, o))
+            piece = dg.at[k, y_of(f) * 2 + side]
+            if (o, k) in ((3, 0), (1, 2)):
+                net.send(("relay", key), piece, piece, me.at_y(1 if o == 3 else -1))
         for k in (0, 2):
             net.send(("core", k, o), dg.at[k, two], dg.at[k + 1, two], me.other_core())
         for k in (0, 2):
@@ -199,7 +198,8 @@
         for way in ("S", "L"):
             net.wait((f, way, len(HOPS[way])))
             value += buffer(f, way, len(HOPS[way]), False)[...].astype(F32)
-        r_ref[:, pl.ds(pl.multiple_of(y_of(f) * CHUNK, CHUNK), CHUNK)] = value
+        start = pl.multiple_of(MARGIN + y_of(f) * CHUNK, CHUNK)
+        response[:, pl.ds(start, CHUNK)] = value
 
     todo = [(f + (hop - 0.5 if hop > 1 else 0), f, hop) for f in range(CHUNKS) for hop in range(1, 6)]
     for _, f, hop in sorted(todo):
@@ -207,19 +207,26 @@
             stage(f, hop)
         else:
             total(f)
-    net.finish()
-
-
-def gather_kernel(o_ref, osh_ref, rows_ref, cols_ref, send_sem, recv_sem):
-    me = Place()
+
+
+def open_loop(response, s_ref, lag_ref, count_ref, o_ref, osh_ref):
+    window = response[...]
+    lag = jnp.full(window.shape, lag_ref[0], jnp.int32)
+    for bit in range(MARGIN.bit_length()):
+        moved = pltpu.roll(window, 1 << bit, 1)
+        window = jnp.where((lag & (1 << bit)) != 0, moved, window)
+    summed = window[:, MARGIN:] + s_ref[...].astype(F32)
+    frame = lax.broadcasted_iota(jnp.int32, summed.shape, 1)
+    count = jnp.full(summed.shape, count_ref[0], jnp.int32)
+    value = jnp.where(frame < count, summed, 0.0).astype(BF)
+    o_ref[...] = value
+    later = pltpu.roll(value.astype(F32), 1, 1)
+    osh_ref[...] = jnp.where(frame == 0, 0.0, later).astype(BF)
+
+
+def gather_slopes(me, net, o_ref, osh_ref, rows_ref, cols_ref):
     r, c, z, xh = me.r, me.c, me.z, me.xh
-    target = ((c + 4) % 8, r * 4 + c // 8)
-    source = (c // 4, (c % 4) * 8 + (r + 4) % 8)
-    greet(
-        [me.other_core(), me.x_near(), me.x_far(), me.at_z(1), me.at_z(-1), me.at_y(1), me.at_y(-1)]
-        + [target, source]
-    )
-    net = Net(send_sem, recv_sem)
+    target = me.permuted()
     first, second = pl.ds(0, 32), pl.ds(32, 32)
     hops = {"L": 4, "S": 3}
     step = {"L": me.sign, "S": -me.sign}
@@ -293,20 +300,43 @@
     for key, entry in net.copies.items():
         if not entry[1]:
             net.wait(key)
+
+
+def kernel(
+    a_ref, d_ref, s_ref, lag_ref, count_ref, rows_ref, cols_ref,
+    response, o_scr, osh_scr, a4, dg, sb, rb, sf, rf, send_sem, recv_sem,
+):
+    me = Place()
+    greet(
+        [me.other_core(), me.x_near(), me.x_far(), me.x_cross(), me.x_far_core(), me.at_z(1), me.at_z(-1)]
+        + [me.at_y(1), me.at_y(-1), me.permuted(), me.permuted_from()]
+    )
+    net = Net(send_sem, recv_sem)
+    response[:, :MARGIN] = jnp.zeros((64, MARGIN), F32)
+    reduce_slopes(me, net, a_ref, d_ref, response, a4, dg, sb, rb, sf, rf)
+    open_loop(response, s_ref, lag_ref, count_ref, o_scr, osh_scr)
+    gather_slopes(me, net, o_scr, osh_scr, rows_ref, cols_ref)
     net.finish()
 
 
-def reduced(interaction, commands):
+def gathered(interaction, commands, slopes_measured, frame_lag, frame_count):
     kinds = [kind for way in HOPS.values() for kind in way]
     n_bf, n_f32 = kinds.count(BF), kinds.count(F32)
     piece = (64, CHUNK)
-    copies = 80
+    copies = 160
+    smem = pl.BlockSpec(memory_space=pltpu.SMEM)
     return pl.pallas_call(
-        reduce_kernel,
-        out_shape=jax.ShapeDtypeStruct((64, FRAMES), F32),
-        in_specs=[VMEM] * 2,
-        out_specs=VMEM,
+        kernel,
+        out_shape=(
+            jax.ShapeDtypeStruct((32, 64, FRAMES), BF),
+            jax.ShapeDtypeStruct((8, 64, FRAMES), BF),
+        ),
+        in_specs=[VMEM, VMEM, VMEM, smem, smem],
+        out_specs=(VMEM, VMEM),
         scratch_shapes=[
+            pltpu.VMEM((64, MARGIN + FRAMES), F32),
+            pltpu.VMEM((64, FRAMES), BF),
+            pltpu.VMEM((64, FRAMES), BF),
             pltpu.VMEM((3, 8, 64, 256), BF),
             pltpu.VMEM((4, 8, 128, 256), BF),
             pltpu.VMEM((CHUNKS, n_bf) + piece, BF),
@@ -316,45 +346,15 @@
             pltpu.SemaphoreType.DMA((copies,)),
             pltpu.SemaphoreType.DMA((copies,)),
         ],
-        compiler_params=pltpu.CompilerParams(collective_id=0, has_side_effects=True),
-        name="reduce_slopes",
-    )(interaction.reshape(2, 8, 2, 64, 256), commands)
-
-
-def gathered(openloop, shifted):
-    return pl.pallas_call(
-        gather_kernel,
-        out_shape=(
-            jax.ShapeDtypeStruct((32, 64, FRAMES), BF),
-            jax.ShapeDtypeStruct((8, 64, FRAMES), BF),
+        compiler_params=pltpu.CompilerParams(
+            collective_id=0, has_side_effects=True, vmem_limit_bytes=24 * 2**20
         ),
-        in_specs=[VMEM] * 2,
-        out_specs=(VMEM, VMEM),
-        scratch_shapes=[pltpu.SemaphoreType.DMA((80,)), pltpu.SemaphoreType.DMA((80,))],
-        compiler_params=pltpu.CompilerParams(collective_id=1, has_side_effects=True),
-        name="gather_slopes",
-    )(openloop, shifted)
-
-
-def delay_frames(response, frame_lag):
-    margin = FRAMES // 4
-    padded = jnp.concatenate(
-        [jnp.zeros((response.shape[0], margin), response.dtype), response], axis=1
-    )
-    return lax.dynamic_slice_in_dim(padded, margin - frame_lag[0], FRAMES, 1)
-
-
-def mask_frames(summed, frame_count):
-    frame_index = lax.broadcasted_iota(jnp.int32, summed.shape, 1)
-    return jnp.where(frame_index < frame_count[0], summed, 0.0).astype(BF)
+        name="open_loop_slopes",
+    )(interaction.reshape(2, 8, 2, 64, 256), commands, slopes_measured, frame_lag, frame_count)
 
 
 def local(interaction, commands, slopes_measured, frame_lag, frame_count):
-    response = reduced(interaction, commands)
-    summed = delay_frames(response, frame_lag) + slopes_measured.astype(F32)
-    openloop = mask_frames(summed, frame_count)
-    shifted = jnp.concatenate([jnp.zeros((64, 1), BF), openloop[:, :-1]], axis=1)
-    rows, cols = gathered(openloop, shifted)
+    rows, cols = gathered(interaction, commands, slopes_measured, frame_lag, frame_count)
     tile = lax.dot_general(
         rows.reshape(2048, FRAMES),
         cols.reshape(512, FRAMES),

time: 109 us -> 101 us (0.927)
  Pallas kernels: 98.3 us -> 92 us
  matrix products: 6.88 us -> 4.4 us
  local copies, waits for them, and re-layouts: 0.76 us -> 2.96 us
  other arithmetic: 1.17 us -> 0 us
    pallas_call x2 -> x1, Pallas kernels: 98.3 us -> 92 us  [gathered(): pl.pallas_call(kernel, out_shape=(jax.ShapeDtypeStruct((32, 64, FRAMES),...]
    unnamed x2 -> x6, local copies, waits for them, and re-layouts: 0.01 us -> 2.96 us
    dot_general x1, matrix products: 6.88 us -> 4.4 us  [local(): lax.dot_general(rows.reshape(2048, FRAMES), cols.reshape(512, FRAMES), ((...]
    convert_element_type x1 -> x0, other arithmetic: 1.17 us -> none  [mask_frames(): return jnp.where(frame_index < frame_count[0], summed, 0.0).astype(BF)]
where the time goes in v3:
time: 101 us
  Pallas kernels  92 us (91%)
  matrix products  4.4 us (4%)
  local copies, waits for them, and re-layouts  2.96 us (3%)
  between operations  1.32 us (1%)
    pallas_call x1, Pallas kernels, gathered(): pl.pallas_call(kernel, out_shape=(jax.ShapeDtypeStruct((32, 64, FRAMES),...  92 us
    dot_general x1, matrix products, local(): lax.dot_general(rows.reshape(2048, FRAMES), cols.reshape(512, FRAMES), ((...  4.4 us
    unnamed x6, local copies, waits for them, and re-layouts  2.96 us

profile of v3, /device:TPU:1, one launch (start us, length us, event | category | flops | bytes accessed | tf_op | source)
XLA Modules:
  0.0 100.7 jit_solution(1502890334707393836)
XLA Ops:
  1.3 0.0 copy-start
  1.3 1.2 %copy-done = bf16[2048,256]{1,0:T(8,128)(2,1)S(1)} copy-done((bf16[2048,256]{1,0:T(8,128)(2,1)S(1)}, bf16[2048,256]{1,0:T(8,128)(2,1)}, u32[]{:S(2)}) %copy-start) | copy-done | bytes 1048600
  2.5 0.0 copy-start.1
  2.5 0.9 copy-done.1
  3.4 0.0 copy-start.2
  3.4 0.8 copy-done.2
  4.3 92.0 %open_loop_slopes.1 = (bf16[32,64,1024]{2,1,0:T(8,128)(2,1)S(1)}, bf16[8,64,1024]{2,1,0:T(8,128)(2,1)S(1)}) custom-call(bf16[2,8,2,64,256]{4,3,2,1,0:T(8,128)(2,1)S(1)} %bitcast.5, bf16[128,256]{1,0:T(8,128)(2,1)S(1)} %copy-done.2, bf16[64,1024]{1,0:T(8,128)(2,1)S(1)} %copy-done.1, s32[1]{0:T(128)S(6)} %copy.6.lag_ref, s32[1]{0:T(128)S(6)} %copy.7.count_ref), custom_call_target="tpu_custom_call" | custom-call | tf_op jit(solution)/shard_map/open_loop_slopes/pallas_call | solution.py:328
  96.3 4.4 %convolution_multiply_fusion = f32[2048,512]{1,0:T(8,128)} fusion(bf16[2048,1024]{1,0:T(8,128)(2,1)S(1)} %bitcast.6, bf16[512,1024]{1,0:T(8,128)(2,1)S(1)} %bitcast.7), kind=kOutput, calls=%fused_computation | convolution fusion | flops 2148532224 | bytes 9437184 | tf_op jit(solution)/shard_map/dot_general | solution.py:358
Async XLA Ops:
  1.3 1.2 %copy-start = (bf16[2048,256]{1,0:T(8,128)(2,1)S(1)}, bf16[2048,256]{1,0:T(8,128)(2,1)}, u32[]{:S(2)}) copy-start(bf16[2048,256]{1,0:T(8,128)(2,1)} %param.5) | copy-start | bytes 3145732
  2.5 0.9 copy-start.1
  3.4 0.8 copy-start.2

commit v4 on v3

--- a/solution.py
+++ b/solution.py
@@ -238,8 +238,19 @@
         piece = rows_ref.at[n, half]
         net.send(key, piece, piece, device)
 
+    near = me.y * 2 + (1 - me.xl)
+    halves = (first, second)
+
+    def to_core(key, n):
+        net.send(key, rows_ref.at[n], rows_ref.at[n], me.other_core())
+
+    def pass_col(key, row, half, device):
+        piece = cols_ref.at[(row + 4) % 8, half]
+        net.send(key, piece, piece, device)
+
     net.send("x1", o_ref.at[first], rows_ref.at[c, first], me.x_far())
-    net.send("permute", osh_ref, cols_ref.at[c % 8], target)
+    for p, half in enumerate(halves):
+        net.send(("permute", p), osh_ref.at[half], cols_ref.at[c % 8, half], target)
     for way in hops:
         net.send(("z2", way, 1), o_ref.at[second], rows_ref.at[c, second], me.at_z(step[way]))
     for way in hops:
@@ -247,56 +258,60 @@
     net.send(("x2", "own", 0), o_ref.at[second], rows_ref.at[c, second], me.x_far())
     net.send("core_own", o_ref, rows_ref.at[c], me.other_core())
     rows_ref[c] = o_ref[...]
-    net.wait("x1")
-    for way in hops:
-        pass_on(("z1p", way, 1), slot(True, 0), first, me.at_z(step[way]))
-
-    def to_core(key, n):
-        net.send(key, rows_ref.at[n], rows_ref.at[n], me.other_core())
-
-    def col_slot(row):
-        return (row + 4) % 8
-
-    def pass_col(key, row, device):
-        piece = cols_ref.at[col_slot(row)]
-        net.send(key, piece, piece, device)
-
-    near = me.y * 2 + (1 - me.xl)
-    for t in range(1, 5):
-        ways = [way for way in hops if t <= hops[way]]
-        for kind, half in (("z2", second), ("z1", first), ("z1p", first)):
-            for way in ways:
-                n = slot(kind == "z1p", -step[way] * t)
-                net.wait((kind, way, t))
-                if t < hops[way]:
-                    pass_on((kind, way, t + 1), n, half, me.at_z(step[way]))
-                if kind == "z2":
-                    pass_on(("x2", way, t), n, second, me.x_far())
-                if kind == "z1":
-                    to_core(("core", way, t), n)
-        if t == 1:
-            net.wait("permute")
-            pass_col("near", r, me.x_near())
-            pass_col(("y0", 1), r, me.at_y(1))
-            pass_col(("y0", -1), r, me.at_y(-1))
-        if t == 2:
-            net.wait("near")
-            pass_col(("y1", 1), near, me.at_y(1))
-            pass_col(("y1", -1), near, me.at_y(-1))
-        if t == 3:
-            net.wait(("y0", 1))
-            pass_col(("y2", 1), (r + 6) % 8, me.at_y(1))
-            net.wait(("y1", -1))
-            pass_col(("y2", -1), (near + 2) % 8, me.at_y(-1))
-    net.wait(("x2", "own", 0))
-    to_core(("core_far", "own", 0), slot(True, 0))
+
+    events = []
+
+    def on(time, key, act=None):
+        events.append((time, len(events), key, act))
+
+    def relay(kind, half, way, t):
+        def act():
+            n = slot(kind == "z1p", -step[way] * t)
+            if t < hops[way]:
+                pass_on((kind, way, t + 1), n, half, me.at_z(step[way]))
+            if kind == "z2":
+                pass_on(("x2", way, t), n, second, me.x_far())
+            if kind == "z1":
+                to_core(("core", way, t), n)
+
+        return act
+
+    def cross_over():
+        for way in hops:
+            pass_on(("z1p", way, 1), slot(True, 0), first, me.at_z(step[way]))
+
+    def far(way, t):
+        n = slot(True, 0 if t == 0 else -step[way] * t)
+        return lambda: to_core(("core_far", way, t), n)
+
+    on(4, "x1", cross_over)
+    on(12, ("x2", "own", 0), far("own", 0))
     for t in range(1, 5):
         for way in hops:
             if t <= hops[way]:
-                net.wait(("x2", way, t))
-                to_core(("core_far", way, t), slot(True, -step[way] * t))
-    for key in [("y0", -1), ("y1", 1), ("y2", 1), ("y2", -1), "core_own"]:
+                on(4 * t, ("z2", way, t), relay("z2", second, way, t))
+                on(4 * t + 1, ("z1", way, t), relay("z1", first, way, t))
+                on(4 * t + 4.5, ("z1p", way, t), relay("z1p", first, way, t))
+                on(4 * t + 7, ("x2", way, t), far(way, t))
+    for p, half in enumerate(halves):
+        def spread(p=p, half=half):
+            pass_col(("near", p), r, half, me.x_near())
+            for d in (1, -1):
+                pass_col(("y0", p, d), r, half, me.at_y(d))
+
+        def spread_near(p=p, half=half):
+            for d in (1, -1):
+                pass_col(("y1", p, d), near, half, me.at_y(d))
+
+        late = 2 * p
+        on(9 + late, ("permute", p), spread)
+        on(13 + late, ("near", p), spread_near)
+        on(14 + late, ("y0", p, 1), lambda p=p, half=half: pass_col(("y2", p, 1), (r + 6) % 8, half, me.at_y(1)))
+        on(18 + late, ("y1", p, -1), lambda p=p, half=half: pass_col(("y2", p, -1), (near + 2) % 8, half, me.at_y(-1)))
+    for _, _, key, act in sorted(events, key=lambda e: e[:2]):
         net.wait(key)
+        if act is not None:
+            act()
     for key, entry in net.copies.items():
         if not entry[1]:
             net.wait(key)

time: 101 us -> 105 us (1.040)
  the two profiles are of different devices: /device:TPU:1 before, /device:TPU:34 now
where the time goes in v4:
time: 105 us
  Pallas kernels  96.3 us (92%)
  matrix products  4.4 us (4%)
  local copies, waits for them, and re-layouts  2.96 us (3%)
  between operations  1.32 us (1%)
    pallas_call x1, Pallas kernels, gathered(): pl.pallas_call(kernel, out_shape=(jax.ShapeDtypeStruct((32, 64, FRAMES),...  96.3 us
    dot_general x1, matrix products, local(): lax.dot_general(rows.reshape(2048, FRAMES), cols.reshape(512, FRAMES), ((...  4.4 us
    unnamed x6, local copies, waits for them, and re-layouts  2.96 us

profile of v4, /device:TPU:34, one launch (start us, length us, event | category | flops | bytes accessed | tf_op | source)
XLA Modules:
  0.0 105.0 jit_solution(7807055451218456318)
XLA Ops:
  1.3 0.0 copy-start
  1.3 1.2 %copy-done = bf16[2048,256]{1,0:T(8,128)(2,1)S(1)} copy-done((bf16[2048,256]{1,0:T(8,128)(2,1)S(1)}, bf16[2048,256]{1,0:T(8,128)(2,1)}, u32[]{:S(2)}) %copy-start) | copy-done | bytes 1048600
  2.5 0.0 copy-start.1
  2.5 0.9 copy-done.1
  3.4 0.0 copy-start.2
  3.4 0.8 copy-done.2
  4.3 96.3 %open_loop_slopes.1 = (bf16[32,64,1024]{2,1,0:T(8,128)(2,1)S(1)}, bf16[8,64,1024]{2,1,0:T(8,128)(2,1)S(1)}) custom-call(bf16[2,8,2,64,256]{4,3,2,1,0:T(8,128)(2,1)S(1)} %bitcast.5, bf16[128,256]{1,0:T(8,128)(2,1)S(1)} %copy-done.2, bf16[64,1024]{1,0:T(8,128)(2,1)S(1)} %copy-done.1, s32[1]{0:T(128)S(6)} %copy.6.lag_ref, s32[1]{0:T(128)S(6)} %copy.7.count_ref), custom_call_target="tpu_custom_call" | custom-call | tf_op jit(solution)/shard_map/open_loop_slopes/pallas_call | solution.py:343
  100.6 4.4 %convolution_multiply_fusion = f32[2048,512]{1,0:T(8,128)} fusion(bf16[2048,1024]{1,0:T(8,128)(2,1)S(1)} %bitcast.6, bf16[512,1024]{1,0:T(8,128)(2,1)S(1)} %bitcast.7), kind=kOutput, calls=%fused_computation | convolution fusion | flops 2148532224 | bytes 9437184 | tf_op jit(solution)/shard_map/dot_general | solution.py:373
Async XLA Ops:
  1.3 1.2 %copy-start = (bf16[2048,256]{1,0:T(8,128)(2,1)S(1)}, bf16[2048,256]{1,0:T(8,128)(2,1)}, u32[]{:S(2)}) copy-start(bf16[2048,256]{1,0:T(8,128)(2,1)} %param.5) | copy-start | bytes 3145732
  2.5 0.9 copy-start.1
  3.4 0.8 copy-start.2

commit v5 on v4

--- a/solution.py
+++ b/solution.py
@@ -16,6 +16,11 @@
 Y_ORDER = (0, 1, 3, 2)
 HOPS = {"L": (BF, BF, F32, F32), "S": (BF, BF, F32)}
 A_ORDER = (("L", 1), ("S", 1), ("L", 2), ("S", 2), ("L", 3), ("S", 3), ("L", 4), ("L", 5))
+
+
+CHUNK_START = (8.5, 12.5, 12.6, 17.0)
+HOP_TIME = 4.0
+COL_LATE = -5.0
 
 
 class Place:
@@ -102,10 +107,10 @@
         hops = len(HOPS[way])
         return (z + (sgn if way == "L" else -sgn) * (hops + 1 - hop) + 16) % 8
 
+    net.send("d_far", d_ref, dg.at[2, r], me.x_far())
     net.send("d_near", d_ref, dg.at[0, r], me.x_near())
     net.send("d_cross", d_ref, dg.at[2, r], me.x_cross())
-    net.send("d_far", d_ref, dg.at[2, r], me.x_far())
-    net.send("d_core", d_ref, dg.at[1, r], me.other_core())
+    net.send(("core", "d", 0), d_ref, dg.at[1, r], me.other_core())
     for o in (1, 3):
         net.send(("d", o), d_ref, dg.at[0, r], me.at_y(-o))
     net.send("a_core", a_ref.at[xh, :, 1 - core], a4.at[0], me.other_core())
@@ -115,35 +120,37 @@
         n = owner(way, hop, -sign)
         net.send(("a_cross", way, hop), a_ref.at[1 - xh, n, 1 - core], a4.at[2, n], me.x_far_core())
     dg[0, r] = d_ref[...]
-    for key, k, row in (("d_near", 0, near), ("d_cross", 2, near), ("d_far", 2, r)):
-        net.wait(key)
-        piece = dg.at[k, row]
-        for o in (1, 3):
-            net.send((key, o), piece, piece, me.at_y(-o))
-        net.send((key, "core"), piece, dg.at[k + 1, row], me.other_core())
-
     def y_of(f):
         return (me.y + Y_ORDER[f]) % 4
 
+    pieces_of = (("d", 0, me.xl), ("d_near", 0, 1 - me.xl), ("d_cross", 2, 1 - me.xl), ("d_far", 2, me.xl))
+
+    def from_x(key, k, row):
+        def act():
+            net.wait(key)
+            piece = dg.at[k, row]
+            for o in (1, 3):
+                net.send((key, o), piece, piece, me.at_y(-o))
+            net.send(("core", key, 0), piece, dg.at[k + 1, row], me.other_core())
+
+        return act
+
+    def from_y(key, k, side, o):
+        def act():
+            net.wait((key, o))
+            row = (me.y + o) % 4 * 2 + side
+            piece = dg.at[k, row]
+            if (o, k) in ((3, 0), (1, 2)):
+                net.send((key, 2), piece, piece, me.at_y(1 if o == 3 else -1))
+            net.send(("core", key, o), piece, dg.at[k + 1, row], me.other_core())
+
+        return act
+
     def commands_in(f):
-        o = Y_ORDER[f]
-        two = pl.ds(y_of(f) * 2, 2)
+        for key, _, _ in pieces_of:
+            net.wait(("core", key, Y_ORDER[f]))
         if f == 0:
-            for key in ("d_core", ("d_near", "core"), ("d_cross", "core"), ("d_far", "core"), "a_core"):
-                net.wait(key)
-            return
-        for key, k, side in (("d", 0, me.xl), ("d_near", 0, 1 - me.xl), ("d_cross", 2, 1 - me.xl), ("d_far", 2, me.xl)):
-            if o == 2:
-                net.wait(("relay", key))
-                continue
-            net.wait((key, o))
-            piece = dg.at[k, y_of(f) * 2 + side]
-            if (o, k) in ((3, 0), (1, 2)):
-                net.send(("relay", key), piece, piece, me.at_y(1 if o == 3 else -1))
-        for k in (0, 2):
-            net.send(("core", k, o), dg.at[k, two], dg.at[k + 1, two], me.other_core())
-        for k in (0, 2):
-            net.wait(("core", k, o))
+            net.wait("a_core")
 
     arrived = set()
 
@@ -201,12 +208,25 @@
         start = pl.multiple_of(MARGIN + y_of(f) * CHUNK, CHUNK)
         response[:, pl.ds(start, CHUNK)] = value
 
-    todo = [(f + (hop - 0.5 if hop > 1 else 0), f, hop) for f in range(CHUNKS) for hop in range(1, 6)]
-    for _, f, hop in sorted(todo):
-        if hop < 5:
-            stage(f, hop)
-        else:
-            total(f)
+    events = []
+
+    def on(time, act):
+        events.append((time, len(events), act))
+
+    on(4.0, from_x("d_near", 0, near))
+    on(4.2, from_x("d_cross", 2, near))
+    on(6.0, from_x("d_far", 2, r))
+    for o in (1, 3):
+        for time, (key, k, side) in zip((4.5, 8.2, 9.0, 11.0), pieces_of):
+            on(time, from_y(key, k, side, o))
+    for time, (key, k, side) in zip((8.4, 12.0, 13.0, 15.0), pieces_of):
+        on(time, from_y(key, k, side, 2))
+    for f, begin in enumerate(CHUNK_START):
+        for hop in range(1, 5):
+            on(begin + HOP_TIME * (hop - 1), lambda f=f, hop=hop: stage(f, hop))
+        on(begin + HOP_TIME * 4, lambda f=f: total(f))
+    for _, _, act in sorted(events, key=lambda e: e[:2]):
+        act()
 
 
 def open_loop(response, s_ref, lag_ref, count_ref, o_ref, osh_ref):
@@ -303,7 +323,7 @@
             for d in (1, -1):
                 pass_col(("y1", p, d), near, half, me.at_y(d))
 
-        late = 2 * p
+        late = 2 * p + COL_LATE
         on(9 + late, ("permute", p), spread)
         on(13 + late, ("near", p), spread_near)
         on(14 + late, ("y0", p, 1), lambda p=p, half=half: pass_col(("y2", p, 1), (r + 6) % 8, half, me.at_y(1)))

time: 105 us -> 94.6 us (0.901)
  the two profiles are of different devices: /device:TPU:34 before, /device:TPU:1 now
where the time goes in v5:
time: 94.6 us; the launch traced here: 93.9 us
  Pallas kernels  85.2 us (90%)
  matrix products  4.4 us (5%)
  local copies, waits for them, and re-layouts  2.96 us (3%)
  between operations  1.32 us (1%)
    pallas_call x1, Pallas kernels, gathered(): pl.pallas_call(kernel, out_shape=(jax.ShapeDtypeStruct((32, 64, FRAMES),...  85.2 us
    dot_general x1, matrix products, local(): lax.dot_general(rows.reshape(2048, FRAMES), cols.reshape(512, FRAMES), ((...  4.4 us
    unnamed x6, local copies, waits for them, and re-layouts  2.96 us

profile of v5, /device:TPU:1, one launch (start us, length us, event | category | flops | bytes accessed | tf_op | source)
XLA Modules:
  0.0 93.9 jit_solution(13328411913635228794)
XLA Ops:
  1.3 0.0 copy-start
  1.3 1.2 %copy-done = bf16[2048,256]{1,0:T(8,128)(2,1)S(1)} copy-done((bf16[2048,256]{1,0:T(8,128)(2,1)S(1)}, bf16[2048,256]{1,0:T(8,128)(2,1)}, u32[]{:S(2)}) %copy-start) | copy-done | bytes 1048600
  2.5 0.0 copy-start.1
  2.5 0.9 copy-done.1
  3.4 0.0 copy-start.2
  3.4 0.8 copy-done.2
  4.3 85.2 %open_loop_slopes.1 = (bf16[32,64,1024]{2,1,0:T(8,128)(2,1)S(1)}, bf16[8,64,1024]{2,1,0:T(8,128)(2,1)S(1)}) custom-call(bf16[2,8,2,64,256]{4,3,2,1,0:T(8,128)(2,1)S(1)} %bitcast.5, bf16[128,256]{1,0:T(8,128)(2,1)S(1)} %copy-done.2, bf16[64,1024]{1,0:T(8,128)(2,1)S(1)} %copy-done.1, s32[1]{0:T(128)S(6)} %copy.6.lag_ref, s32[1]{0:T(128)S(6)} %copy.7.count_ref), custom_call_target="tpu_custom_call" | custom-call | tf_op jit(solution)/shard_map/open_loop_slopes/pallas_call | solution.py:363
  89.5 4.4 %convolution_multiply_fusion = f32[2048,512]{1,0:T(8,128)} fusion(bf16[2048,1024]{1,0:T(8,128)(2,1)S(1)} %bitcast.6, bf16[512,1024]{1,0:T(8,128)(2,1)S(1)} %bitcast.7), kind=kOutput, calls=%fused_computation | convolution fusion | flops 2148532224 | bytes 9437184 | tf_op jit(solution)/shard_map/dot_general | solution.py:393
Async XLA Ops:
  1.3 1.2 %copy-start = (bf16[2048,256]{1,0:T(8,128)(2,1)S(1)}, bf16[2048,256]{1,0:T(8,128)(2,1)}, u32[]{:S(2)}) copy-start(bf16[2048,256]{1,0:T(8,128)(2,1)} %param.5) | copy-start | bytes 3145732
  2.5 0.9 copy-start.1
  3.4 0.8 copy-start.2
